TPU v7x, 256 devices: a whole 4x4x8 slice. The times are simulated.
256 devices in a mesh: dp: 8 (over z_hi, core), expert: 32 (over x, z_lo, y).
Axes of the slice: x: 4, y: 4, z: 8 (z_hi: 4, z_lo: 2; z = z_hi * 2 + z_lo), core: 2. Of those that a mesh axis runs over, the one named last changes fastest.
Arguments:
- tokens: bfloat16 [256, 256, 1024], P(('dp', 'expert'))
- router: bfloat16 [1024, 128], replicated
- weight_in: bfloat16 [128, 1024, 2048], P('expert', None, 'dp'), may hold values from -0.1875 to 0.1875
- weight_out: bfloat16 [128, 2048, 1024], P('expert', 'dp'), may hold values from -0.125 to 0.125
- cotangent: bfloat16 [256, 256, 1024], P(('dp', 'expert')), may hold values from -6 to 6
Outputs:
- mixed: bfloat16 [256, 256, 1024], P(('dp', 'expert'))
- grad_tokens: bfloat16 [256, 256, 1024], P(('dp', 'expert'))
- grad_router: float32 [1024, 128], replicated
- grad_weight_in: bfloat16 [128, 1024, 2048], P('expert', None, 'dp')
- grad_weight_out: bfloat16 [128, 2048, 1024], P('expert', 'dp')
All inputs are finite; a program needn't handle non-finite values.
Results may differ from a plain program's by a relative error of at most 0.018.
Values may be sent and summed in bfloat16 or wider, within the bound.
A program may use at most 64 MiB of HBM per device.

v0:
```python
import jax
import jax.numpy as jnp
from jax import lax
from jax.sharding import PartitionSpec as P


def gelu_exact(values):
    return jax.nn.gelu(values, approximate=False)


def local(tokens, router, weight_in, weight_out, cotangent):
    experts_dev = weight_in.shape[0]
    width = tokens.shape[2]
    logits = jnp.einsum("isd,de->ise", tokens, router, preferred_element_type=jnp.float32)
    dispatch_prob = jax.nn.softmax(logits, axis=1)
    combine_prob = jax.nn.softmax(logits, axis=2)
    dispatch = dispatch_prob.astype(jnp.bfloat16)
    combine = combine_prob.astype(jnp.bfloat16)
    slots = jnp.einsum("ise,isd->ied", dispatch, tokens, preferred_element_type=jnp.float32).astype(
        jnp.bfloat16
    )
    grad_slots = jnp.einsum(
        "ise,isd->ied", combine, cotangent, preferred_element_type=jnp.float32
    ).astype(jnp.bfloat16)

    def to_owners(local_rows):
        arrived = lax.all_to_all(local_rows, "expert", split_axis=1, concat_axis=1, tiled=True)
        return lax.all_gather(arrived, "dp", axis=0, tiled=True)

    def from_owners(partial_value):
        summed = lax.psum_scatter(partial_value, "dp", scatter_dimension=0, tiled=True).astype(
            jnp.float32
        )
        return lax.all_to_all(
            summed.astype(jnp.bfloat16), "expert", split_axis=1, concat_axis=1, tiled=True
        )

    slot_rows = to_owners(slots)
    blocks = slot_rows.reshape(-1, experts_dev, width)
    pre_act = jnp.einsum("rkd,kdf->rkf", blocks, weight_in, preferred_element_type=jnp.float32)
    hidden = gelu_exact(pre_act).astype(jnp.bfloat16)
    partial_value = jnp.einsum(
        "rkf,kfd->rkd", hidden, weight_out, preferred_element_type=jnp.float32
    )
    blocks, pre_act, hidden, partial_value = (
        blocks,
        pre_act,
        hidden,
        partial_value.astype(jnp.bfloat16).reshape(slot_rows.shape),
    )
    expert_outs = from_owners(partial_value)
    grad_rows = to_owners(grad_slots)
    grad_blocks = grad_rows.reshape(blocks.shape)
    grad_hidden = jnp.einsum(
        "rkd,kfd->rkf", grad_blocks, weight_out, preferred_element_type=jnp.float32
    )
    _, gelu_back = jax.vjp(gelu_exact, pre_act)
    grad_pre = gelu_back(grad_hidden)[0].astype(jnp.bfloat16)
    grad_second = jnp.einsum(
        "rkf,rkd->kfd", hidden, grad_blocks, preferred_element_type=jnp.float32
    ).astype(jnp.bfloat16)
    grad_first = jnp.einsum(
        "rkd,rkf->kdf", blocks, grad_pre, preferred_element_type=jnp.float32
    ).astype(jnp.bfloat16)
    partial_back = jnp.einsum(
        "rkf,kdf->rkd", grad_pre, weight_in, preferred_element_type=jnp.float32
    )
    grad_first, grad_second, partial_back = (
        grad_first,
        grad_second,
        partial_back.astype(jnp.bfloat16).reshape(grad_rows.shape),
    )
    grad_slot_all = from_owners(partial_back)
    mixed = jnp.einsum(
        "ise,ied->isd", combine, expert_outs, preferred_element_type=jnp.float32
    ).astype(jnp.bfloat16)
    grad_comb = jnp.einsum(
        "isd,ied->ise", cotangent, expert_outs, preferred_element_type=jnp.float32
    )
    grad_disp = jnp.einsum(
        "isd,ied->ise", tokens, grad_slot_all, preferred_element_type=jnp.float32
    )
    part_disp = dispatch_prob * (
        grad_disp - jnp.sum(dispatch_prob * grad_disp, axis=1, keepdims=True)
    )
    part_comb = combine_prob * (
        grad_comb - jnp.sum(combine_prob * grad_comb, axis=2, keepdims=True)
    )
    grad_logits = (part_disp + part_comb).astype(jnp.bfloat16)
    grad_tokens = (
        jnp.einsum("ise,ied->isd", dispatch, grad_slot_all, preferred_element_type=jnp.float32)
        + jnp.einsum("ise,de->isd", grad_logits, router, preferred_element_type=jnp.float32)
    ).astype(jnp.bfloat16)
    router_term = jnp.einsum("isd,ise->de", tokens, grad_logits, preferred_element_type=jnp.float32)
    grad_router = lax.psum(router_term, ("dp", "expert"))
    return (mixed, grad_tokens, grad_router, grad_first, grad_second)


def solution(mesh):
    return jax.shard_map(
        local,
        mesh=mesh,
        in_specs=(
            P(("dp", "expert"), None, None),
            P(),
            P("expert", None, "dp"),
            P("expert", "dp", None),
            P(("dp", "expert"), None, None),
        ),
        out_specs=(
            P(("dp", "expert"), None, None),
            P(("dp", "expert"), None, None),
            P(),
            P("expert", None, "dp"),
            P("expert", "dp", None),
        ),
        check_vma=False,
    )
```

profile of v0, /device:TPU:2, one launch (start us, length us, event | category | flops | bytes accessed | tf_op | source)
XLA Modules:
  0.0 497.0 jit_solution(17294189357701382762)
XLA Ops:
  7.2 0.0 all-gather.3.cloned.1.call-start
  7.2 1.6 fusion.62
  8.8 0.2 fusion.47
  9.0 1.3 fusion.9
  10.4 0.4 copy.95
  10.8 0.5 broadcast.298
  11.3 2.1 reduce.12
  13.4 0.2 reshape.119
  13.6 16.7 %all_to_all.20 = bf16[32,2,2048]{2,1,0:T(2,128)(2,1)S(1)} all-to-all(bf16[32,2,2048]{2,1,0:T(2,128)(2,1)S(1)} %reshape.119), channel_id=1, replica_groups=mesh['dp'=8,'expert'=32] {'expert'}, dimensions={0} | all-to-all | bytes 524288 | tf_op jit(solution)/shard_map/all_to_all | solution.py:27
  30.4 0.3 reshape.120
  30.6 0.8 copy.42
  31.4 0.0 all-gather.3.cloned.1.call-update
  31.4 0.0 all-gather.5.cloned.1.call-start
  31.5 0.4 fusion.10
  31.9 0.4 copy.93
  32.3 2.2 reduce.14
  34.5 0.2 reshape.123
  34.6 12.8 %all_to_all.21 = bf16[32,2,2048]{2,1,0:T(2,128)(2,1)S(1)} all-to-all(bf16[32,2,2048]{2,1,0:T(2,128)(2,1)S(1)} %reshape.123), channel_id=1, replica_groups=mesh['dp'=8,'expert'=32] {'expert'}, dimensions={0} | all-to-all | bytes 524288 | tf_op jit(solution)/shard_map/all_to_all | solution.py:27
  47.4 0.3 reshape.124
  47.7 0.8 copy.47
  48.5 0.0 all-gather.5.cloned.1.call-update
  48.5 0.2 reduce-scatter.5.cloned.1.call-start
  48.7 18.3 %all-gather.3.cloned.1.call-done = bf16[8,128,1024]{2,1,0:T(8,128)(2,1)} async-done(((bf16[1,128,1024]{2,1,0:T(8,128)(2,1)}), bf16[8,128,1024]{2,1,0:T(8,128)(2,1)}) %all-gather.3.cloned.1.call-update) | async-done | bytes 2097168 | tf_op jit(solution)/shard_map/all_gather | solution.py:28
  67.0 4.1 reshape.112
  71.1 4.3 copy.53
  75.4 5.3 %fusion.13 = (bf16[256,4,256]{2,0,1:T(8,128)(2,1)S(1)}, f32[4,256,256]{2,1,0:T(8,128)}) fusion(bf16[256,4,1024]{0,2,1:T(8,128)(2,1)} %copy.53, bf16[4,1024,256]{2,1,0:T(8,128)(2,1)S(1)} %copy-done), kind=kOutput, calls=%fused_computation.29 | convolution fusion | flops 553910272 | bytes 5767168 | tf_op jit(solution)/shard_map/rkd,kdf->rkf/dot_general | solution.py:40
  80.7 23.0 %all-gather.5.cloned.1.call-done = bf16[8,128,1024]{2,1,0:T(8,128)(2,1)} async-done(((bf16[1,128,1024]{2,1,0:T(8,128)(2,1)}), bf16[8,128,1024]{2,1,0:T(8,128)(2,1)}) %all-gather.5.cloned.1.call-update) | async-done | bytes 2097168 | tf_op jit(solution)/shard_map/all_gather | solution.py:28
  103.7 4.1 reshape.116
  107.8 5.7 %fusion.19 = bf16[256,4,256]{2,0,1:T(8,128)(2,1)S(1)} fusion(bf16[4,256,1024]{2,1,0:T(8,128)(2,1)} %param.8, bf16[256,4,1024]{2,1,0:T(4,128)(2,1)} %reshape.116, f32[4,256,256]{2,1,0:T(8,128)} %get-tuple-element.33), kind=kOutput, calls=%fused_computation.35 | convolution fusion | flops 555745280 | bytes 5767168 | tf_op jit(solution)/shard_map/rkd,kfd->rkf/dot_general | solution.py:54
  113.6 0.7 convert_bitcast_fusion
  114.3 2.9 copy.49
  117.2 4.0 reshape.117
  121.2 0.0 reduce-scatter.5.cloned.1.call-update
  121.2 0.3 reduce-scatter.3.cloned.1.call-start
  121.5 2.3 convert_bitcast_fusion.1
  123.8 2.9 copy.44
  126.8 3.9 reshape.113
  130.7 0.0 reduce-scatter.3.cloned.1.call-update
  130.7 31.9 %reduce-scatter.5.cloned.1.call-done = bf16[1,128,1024]{2,1,0:T(8,128)(2,1)} async-done(((bf16[8,128,1024]{2,1,0:T(8,128)(2,1)}), bf16[1,128,1024]{2,1,0:T(8,128)(2,1)}) %reduce-scatter.5.cloned.1.call-update) | async-done | bytes 262160 | tf_op jit(solution)/shard_map/reduce_scatter | solution.py:31
  162.6 2.1 copy.92
  164.8 3.1 reduce.15
  167.9 0.9 reshape.125
  168.8 7.7 %all-to-all-start.3 = ((bf16[32,2,2048]{2,1,0:T(2,128)(2,1)}), bf16[32,2,2048]{2,1,0:T(2,128)(2,1)S(1)}, u32[]{:S(2)}, u32[]{:S(2)}) async-start(bf16[32,2,2048]{2,1,0:T(2,128)(2,1)} %reshape.125), calls=%async_computation.5 | async-start | bytes 524288 | tf_op jit(solution)/shard_map/all_to_all | solution.py:34
  176.5 4.5 convolution_convert_fusion
  181.0 28.3 %reduce-scatter.3.cloned.1.call-done = bf16[1,128,1024]{2,1,0:T(8,128)(2,1)} async-done(((bf16[8,128,1024]{2,1,0:T(8,128)(2,1)}), bf16[1,128,1024]{2,1,0:T(8,128)(2,1)}) %reduce-scatter.3.cloned.1.call-update) | async-done | bytes 262160 | tf_op jit(solution)/shard_map/reduce_scatter | solution.py:31
  209.3 1.4 copy.94
  210.7 2.9 reduce.13
  213.5 1.8 reshape.121
  215.4 7.4 %all-to-all-start.1 = ((bf16[32,2,2048]{2,1,0:T(2,128)(2,1)}), bf16[32,2,2048]{2,1,0:T(2,128)(2,1)}, u32[]{:S(2)}, u32[]{:S(2)}) async-start(bf16[32,2,2048]{2,1,0:T(2,128)(2,1)} %reshape.121), calls=%async_computation.2 | async-start | bytes 524288 | tf_op jit(solution)/shard_map/all_to_all | solution.py:34
  222.8 0.3 all-reduce.2.cloned.1.call-start
  223.1 3.6 convolution_convert_fusion.1
  226.7 1.0 reshape.126
  227.7 1.4 fusion.42
  229.0 1.8 all-to-all-done.1
  230.8 2.8 reshape.122
  233.6 1.6 convolution_bitcast_fusion.1
  235.2 1.6 multiply_reduce_fusion.1
  236.8 0.6 copy-done.5
  237.5 1.2 convolution_bitcast_fusion
  238.7 0.0 all-reduce.2.cloned.1.call-update
  238.7 2.2 fusion.7
  240.9 2.2 fusion.8
  243.1 245.3 %all-reduce.2.cloned.1.call-done = f32[1024,128]{0,1:T(8,128)} async-done(((f32[1024,128]{0,1:T(8,128)}), f32[1024,128]{0,1:T(8,128)}) %all-reduce.2.cloned.1.call-update) | async-done | bytes 524304 | tf_op jit(solution)/shard_map/psum | solution.py:95
  488.4 2.0 copy.56
  (16 shorter events, 0.0 us)
Async XLA Ops:
  7.2 68.3 %copy-start = (bf16[4,1024,256]{2,1,0:T(8,128)(2,1)S(1)}, bf16[4,1024,256]{2,1,0:T(8,128)(2,1)}, u32[]{:S(2)}) copy-start(bf16[4,1024,256]{2,1,0:T(8,128)(2,1)} %param.7) | copy-start | bytes 6291460
  7.2 59.8 %all-gather.3.cloned.1.call-start = ((), (), s32[]{:S(2)}) async-start(), calls=%async_computation.6 | async-start | bytes 2359296 | tf_op jit(solution)/shard_map/all_gather | solution.py:28
  10.4 21.1 %copy-start.1 = (bf16[1,256,1024]{2,1,0:T(8,128)(2,1)S(1)}, bf16[1,256,1024]{2,1,0:T(8,128)(2,1)}, u32[]{:S(2)}) copy-start(bf16[1,256,1024]{2,1,0:T(8,128)(2,1)} %param.9) | copy-start | bytes 1572868
  31.4 72.2 %all-gather.5.cloned.1.call-start = ((), (), s32[]{:S(2)}) async-start(), calls=%async_computation.8 | async-start | bytes 2359296 | tf_op jit(solution)/shard_map/all_gather | solution.py:28
  48.5 114.1 %reduce-scatter.5.cloned.1.call-start = ((), (), s32[]{:S(2)}) async-start(), calls=%async_computation.9 | async-start | bytes 2359296 | tf_op jit(solution)/shard_map/reduce_scatter | solution.py:31
  121.2 88.1 %reduce-scatter.3.cloned.1.call-start = ((), (), s32[]{:S(2)}) async-start(), calls=%async_computation.7 | async-start | bytes 2359296 | tf_op jit(solution)/shard_map/reduce_scatter | solution.py:31
  168.8 46.6 %all-to-all-start.3 = ((bf16[32,2,2048]{2,1,0:T(2,128)(2,1)}), bf16[32,2,2048]{2,1,0:T(2,128)(2,1)S(1)}, u32[]{:S(2)}, u32[]{:S(2)}) async-start(bf16[32,2,2048]{2,1,0:T(2,128)(2,1)} %reshape.125), calls=%async_computation.5 | async-start | bytes 524288 | tf_op jit(solution)/shard_map/all_to_all | solution.py:34
  215.4 15.4 %all-to-all-start.1 = ((bf16[32,2,2048]{2,1,0:T(2,128)(2,1)}), bf16[32,2,2048]{2,1,0:T(2,128)(2,1)}, u32[]{:S(2)}, u32[]{:S(2)}) async-start(bf16[32,2,2048]{2,1,0:T(2,128)(2,1)} %reshape.121), calls=%async_computation.2 | async-start | bytes 524288 | tf_op jit(solution)/shard_map/all_to_all | solution.py:34
  222.8 265.6 %all-reduce.2.cloned.1.call-start = ((), (), s32[]{:S(2)}) async-start(), calls=%async_computation.10 | async-start | bytes 1048576 | tf_op jit(solution)/shard_map/psum | solution.py:95
  233.6 3.9 copy-start.2
  235.2 1.6 copy-start.4
  235.2 5.7 %copy-start.3 = (bf16[1024,128]{1,0:T(8,128)(2,1)S(1)}, bf16[1024,128]{1,0:T(8,128)(2,1)}, u32[]{:S(2)}) copy-start(bf16[1024,128]{1,0:T(8,128)(2,1)} %param.6) | copy-start | bytes 786436
  236.8 0.7 copy-start.5
  236.8 0.7 copy-start.6
  236.8 0.6 copy-start.7
Sparse Core Ops, SparseCore 0:
  31.6 35.4 all-gather.2
  69.5 34.1 all-gather.4
  121.4 41.2 reduce-scatter.4
  165.6 43.6 reduce-scatter.2
  238.8 249.5 all-reduce.1
where the time goes:
time: 498 us; the launch traced here: 497 us
  waiting for transfers between devices  349 us (70%)
  local copies, waits for them, and re-layouts  42.7 us (9%)
  matrix products  35.6 us (7%)
  blocking collectives  29.5 us (6%)
  starting transfers between devices  16 us (3%)
  between operations  14 us (3%)
  other arithmetic  10.5 us (2%)
    psum x1, waiting for transfers between devices, local(): grad_router = lax.psum(router_term, ('dp', 'expert'))  245 us
    reduce_scatter x2, waiting for transfers between devices, from_owners(): lax.psum_scatter(partial_value, 'dp', scatter_dimension=0, tiled=True)  60.2 us
    all_gather x2, waiting for transfers between devices, to_owners(): return lax.all_gather(arrived, 'dp', axis=0, tiled=True)  41.3 us
    all_to_all x2, blocking collectives, to_owners(): lax.all_to_all(local_rows, 'expert', split_axis=1, concat_axis=1, tiled=T...  29.5 us
    all_to_all x2, starting transfers between devices, from_owners(): lax.all_to_all(summed.astype(jnp.bfloat16), 'expert', split_axis=1, conca...  15.1 us
    unnamed x26, local copies, waits for them, and re-layouts  10.5 us
    unnamed x4, other arithmetic  10.3 us
  transfers between devices with their start and end apart: 7, of which 6 were waited for; matrix products, arithmetic and copies ran while one was open for 11% of the time, Pallas kernels for 0%

commit v1 on v0

--- a/solution.py
+++ b/solution.py
@@ -92,7 +92,7 @@
         + jnp.einsum("ise,de->isd", grad_logits, router, preferred_element_type=jnp.float32)
     ).astype(jnp.bfloat16)
     router_term = jnp.einsum("isd,ise->de", tokens, grad_logits, preferred_element_type=jnp.float32)
-    grad_router = lax.psum(router_term, ("dp", "expert"))
+    grad_router = jax.lax.psum(jax.lax.psum(router_term, "dp"), "expert")
     return (mixed, grad_tokens, grad_router, grad_first, grad_second)
 
 

time: 498 us -> 616 us (1.24); the launches traced: 497 us -> 606 us
  waiting for transfers between devices: 349 us -> 459 us
    psum x1 -> x2, waiting for transfers between devices: 245 us -> 363 us  [local(): grad_router = jax.lax.psum(jax.lax.psum(router_term, 'dp'), 'expert')]
    all_gather x2, waiting for transfers between devices: 41.3 us -> 33.4 us  [to_owners(): return lax.all_gather(arrived, 'dp', axis=0, tiled=True)]
  transfers between devices with their start and end apart: 7 -> 8, of which waited for: 6 -> 7; matrix products, arithmetic and copies ran while one was open for 11% -> 12% of each run, Pallas kernels for 0% -> 0%
where the time goes in v1:
time: 616 us; the launch traced here: 606 us
  waiting for transfers between devices  459 us (75%)
  local copies, waits for them, and re-layouts  43.5 us (7%)
  matrix products  31.6 us (5%)
  blocking collectives  29.5 us (5%)
  starting transfers between devices  16.4 us (3%)
  between operations  14.3 us (2%)
  other arithmetic  11.6 us (2%)
    psum x2, waiting for transfers between devices, local(): grad_router = jax.lax.psum(jax.lax.psum(router_term, 'dp'), 'expert')  363 us
    reduce_scatter x2, waiting for transfers between devices, from_owners(): lax.psum_scatter(partial_value, 'dp', scatter_dimension=0, tiled=True)  58.2 us
    all_gather x2, waiting for transfers between devices, to_owners(): return lax.all_gather(arrived, 'dp', axis=0, tiled=True)  33.4 us
    all_to_all x2, blocking collectives, to_owners(): lax.all_to_all(local_rows, 'expert', split_axis=1, concat_axis=1, tiled=T...  29.5 us
    all_to_all x2, starting transfers between devices, from_owners(): lax.all_to_all(summed.astype(jnp.bfloat16), 'expert', split_axis=1, conca...  15.5 us
  transfers between devices with their start and end apart: 8, of which 7 were waited for; matrix products, arithmetic and copies ran while one was open for 12% of the time, Pallas kernels for 0%

profile of v1, /device:TPU:2, one launch (start us, length us, event | category | flops | bytes accessed | tf_op | source)
XLA Modules:
  0.0 606.4 jit_solution(9297212298693709992)
XLA Ops:
  7.2 0.0 all-gather.3.cloned.1.call-start
  7.2 1.6 fusion.62
  8.8 0.2 fusion.47
  9.0 1.3 fusion.9
  10.4 0.4 copy.95
  10.8 0.6 broadcast.298
  11.4 2.2 reduce.12
  13.5 0.2 reshape.119
  13.7 16.7 %all_to_all.20 = bf16[32,2,2048]{2,1,0:T(2,128)(2,1)S(1)} all-to-all(bf16[32,2,2048]{2,1,0:T(2,128)(2,1)S(1)} %reshape.119), channel_id=1, replica_groups=mesh['dp'=8,'expert'=32] {'expert'}, dimensions={0} | all-to-all | bytes 524288 | tf_op jit(solution)/shard_map/all_to_all | solution.py:27
  30.5 0.3 reshape.120
  30.7 0.8 copy.42
  31.5 0.0 all-gather.3.cloned.1.call-update
  31.5 0.0 all-gather.5.cloned.1.call-start
  31.6 0.4 fusion.10
  32.0 0.4 copy.93
  32.4 2.2 reduce.14
  34.6 0.2 reshape.123
  34.8 12.8 %all_to_all.21 = bf16[32,2,2048]{2,1,0:T(2,128)(2,1)S(1)} all-to-all(bf16[32,2,2048]{2,1,0:T(2,128)(2,1)S(1)} %reshape.123), channel_id=1, replica_groups=mesh['dp'=8,'expert'=32] {'expert'}, dimensions={0} | all-to-all | bytes 524288 | tf_op jit(solution)/shard_map/all_to_all | solution.py:27
  47.5 0.3 reshape.124
  47.8 0.8 copy.47
  48.6 0.0 all-gather.5.cloned.1.call-update
  48.6 0.2 reduce-scatter.3.cloned.1.call-start
  48.8 18.3 %all-gather.3.cloned.1.call-done = bf16[8,128,1024]{2,1,0:T(8,128)(2,1)} async-done(((bf16[1,128,1024]{2,1,0:T(8,128)(2,1)}), bf16[8,128,1024]{2,1,0:T(8,128)(2,1)}) %all-gather.3.cloned.1.call-update) | async-done | bytes 2097168 | tf_op jit(solution)/shard_map/all_gather | solution.py:28
  67.1 4.1 reshape.112
  71.2 4.3 copy.53
  75.5 5.5 fusion.13
  81.0 0.7 convert_bitcast_fusion.1
  81.7 2.9 copy.44
  84.7 4.0 reshape.113
  88.7 0.3 reduce-scatter.5.cloned.1.call-start
  88.9 15.1 %all-gather.5.cloned.1.call-done = bf16[8,128,1024]{2,1,0:T(8,128)(2,1)} async-done(((bf16[1,128,1024]{2,1,0:T(8,128)(2,1)}), bf16[8,128,1024]{2,1,0:T(8,128)(2,1)}) %all-gather.5.cloned.1.call-update) | async-done | bytes 2097168 | tf_op jit(solution)/shard_map/all_gather | solution.py:28
  104.0 4.1 reshape.116
  108.1 5.7 fusion.19
  113.9 0.7 convert_bitcast_fusion
  114.6 2.9 copy.49
  117.6 4.0 reshape.117
  121.5 0.0 reduce-scatter.5.cloned.1.call-update
  121.5 26.2 %reduce-scatter.3.cloned.1.call-done = bf16[1,128,1024]{2,1,0:T(8,128)(2,1)} async-done(((bf16[8,128,1024]{2,1,0:T(8,128)(2,1)}), bf16[1,128,1024]{2,1,0:T(8,128)(2,1)}) %reduce-scatter.3.cloned.1.call-update) | async-done | bytes 262160 | tf_op jit(solution)/shard_map/reduce_scatter | solution.py:31
  147.8 2.1 copy.94
  149.9 3.2 reduce.13
  153.1 0.9 reshape.121
  153.9 7.3 %all-to-all-start.1 = ((bf16[32,2,2048]{2,1,0:T(2,128)(2,1)}), bf16[32,2,2048]{2,1,0:T(2,128)(2,1)S(1)}, u32[]{:S(2)}, u32[]{:S(2)}) async-start(bf16[32,2,2048]{2,1,0:T(2,128)(2,1)} %reshape.121), calls=%async_computation.2 | async-start | bytes 524288 | tf_op jit(solution)/shard_map/all_to_all | solution.py:34
  161.3 32.0 %reduce-scatter.5.cloned.1.call-done = bf16[1,128,1024]{2,1,0:T(8,128)(2,1)} async-done(((bf16[8,128,1024]{2,1,0:T(8,128)(2,1)}), bf16[1,128,1024]{2,1,0:T(8,128)(2,1)}) %reduce-scatter.5.cloned.1.call-update) | async-done | bytes 262160 | tf_op jit(solution)/shard_map/reduce_scatter | solution.py:31
  193.2 2.1 copy.92
  195.4 3.9 reduce.15
  199.3 1.8 reshape.125
  201.1 8.2 %all-to-all-start.3 = ((bf16[32,2,2048]{2,1,0:T(2,128)(2,1)}), bf16[32,2,2048]{2,1,0:T(2,128)(2,1)}, u32[]{:S(2)}, u32[]{:S(2)}) async-start(bf16[32,2,2048]{2,1,0:T(2,128)(2,1)} %reshape.125), calls=%async_computation.5 | async-start | bytes 524288 | tf_op jit(solution)/shard_map/all_to_all | solution.py:34
  209.3 0.3 all-reduce.3.cloned.1.call-start
  209.6 1.0 reshape.122
  210.5 1.5 convolution_bitcast_fusion.1
  212.1 5.2 all-to-all-done.3
  217.3 2.8 reshape.126
  220.1 1.5 multiply_reduce_fusion.1
  221.6 0.6 copy-done.6
  222.2 2.2 convolution_bitcast_fusion
  224.5 0.0 all-reduce.5.cloned.1.call-start
  224.5 4.6 convolution_convert_fusion
  229.2 2.0 convolution_convert_fusion.1
  231.2 62.8 %all-reduce.3.cloned.1.call-done = f32[1024,128]{0,1:T(8,128)} async-done(((f32[1024,128]{0,1:T(8,128)}), f32[1024,128]{0,1:T(8,128)}) %all-reduce.3.cloned.1.call-update) | async-done | bytes 524304 | tf_op jit(solution)/shard_map/psum | solution.py:95
  294.1 1.2 fusion.7
  295.2 1.4 fusion.42
  296.6 1.2 fusion.8
  297.8 299.7 %all-reduce.5.cloned.1.call-done = f32[1024,128]{0,1:T(8,128)} async-done(((f32[1024,128]{0,1:T(8,128)}), f32[1024,128]{0,1:T(8,128)}) %all-reduce.5.cloned.1.call-update) | async-done | bytes 524304 | tf_op jit(solution)/shard_map/psum | solution.py:95
  597.5 2.0 copy.56
  (23 shorter events, 0.1 us)
Async XLA Ops:
  7.2 68.3 %copy-start = (bf16[4,1024,256]{2,1,0:T(8,128)(2,1)S(1)}, bf16[4,1024,256]{2,1,0:T(8,128)(2,1)}, u32[]{:S(2)}) copy-start(bf16[4,1024,256]{2,1,0:T(8,128)(2,1)} %param.7) | copy-start | bytes 6291460
  7.2 59.9 %all-gather.3.cloned.1.call-start = ((), (), s32[]{:S(2)}) async-start(), calls=%async_computation.6 | async-start | bytes 2359296 | tf_op jit(solution)/shard_map/all_gather | solution.py:28
  10.4 21.2 %copy-start.2 = (bf16[1,256,1024]{2,1,0:T(8,128)(2,1)S(1)}, bf16[1,256,1024]{2,1,0:T(8,128)(2,1)}, u32[]{:S(2)}) copy-start(bf16[1,256,1024]{2,1,0:T(8,128)(2,1)} %param.9) | copy-start | bytes 1572868
  31.5 72.5 %all-gather.5.cloned.1.call-start = ((), (), s32[]{:S(2)}) async-start(), calls=%async_computation.8 | async-start | bytes 2359296 | tf_op jit(solution)/shard_map/all_gather | solution.py:28
  48.6 99.2 %reduce-scatter.3.cloned.1.call-start = ((), (), s32[]{:S(2)}) async-start(), calls=%async_computation.7 | async-start | bytes 2359296 | tf_op jit(solution)/shard_map/reduce_scatter | solution.py:31
  75.5 5.5 copy-start.4
  88.7 104.6 %reduce-scatter.5.cloned.1.call-start = ((), (), s32[]{:S(2)}) async-start(), calls=%async_computation.9 | async-start | bytes 2359296 | tf_op jit(solution)/shard_map/reduce_scatter | solution.py:31
  153.9 47.1 %all-to-all-start.1 = ((bf16[32,2,2048]{2,1,0:T(2,128)(2,1)}), bf16[32,2,2048]{2,1,0:T(2,128)(2,1)S(1)}, u32[]{:S(2)}, u32[]{:S(2)}) async-start(bf16[32,2,2048]{2,1,0:T(2,128)(2,1)} %reshape.121), calls=%async_computation.2 | async-start | bytes 524288 | tf_op jit(solution)/shard_map/all_to_all | solution.py:34
  201.1 16.2 %all-to-all-start.3 = ((bf16[32,2,2048]{2,1,0:T(2,128)(2,1)}), bf16[32,2,2048]{2,1,0:T(2,128)(2,1)}, u32[]{:S(2)}, u32[]{:S(2)}) async-start(bf16[32,2,2048]{2,1,0:T(2,128)(2,1)} %reshape.125), calls=%async_computation.5 | async-start | bytes 524288 | tf_op jit(solution)/shard_map/all_to_all | solution.py:34
  209.3 84.8 %all-reduce.3.cloned.1.call-start = ((), (), s32[]{:S(2)}) async-start(), calls=%async_computation.10 | async-start | bytes 1048576 | tf_op jit(solution)/shard_map/psum | solution.py:95
  221.6 0.6 copy-start.6
  221.6 0.6 copy-start.8
  224.5 373.1 %all-reduce.5.cloned.1.call-start = ((), (), s32[]{:S(2)}) async-start(), calls=%async_computation.11 | async-start | bytes 1048576 | tf_op jit(solution)/shard_map/psum | solution.py:95
  224.5 4.7 copy-start.1
  229.2 64.9 %copy-start.3 = (bf16[128,1,1024]{2,1,0:T(2,128)(2,1)S(1)}, bf16[128,1,1024]{2,1,0:T(2,128)(2,1)}, u32[]{:S(2)}) copy-start(bf16[128,1,1024]{2,1,0:T(2,128)(2,1)} %reshape.122) | copy-start | bytes 786436
  231.2 65.4 %copy-start.5 = (bf16[1024,128]{1,0:T(8,128)(2,1)S(1)}, bf16[1024,128]{1,0:T(8,128)(2,1)}, u32[]{:S(2)}) copy-start(bf16[1024,128]{1,0:T(8,128)(2,1)} %param.6) | copy-start | bytes 786436
  231.2 65.4 %copy-start.7 = (f32[256]{0:T(256)S(1)}, f32[256]{0:T(256)}, u32[]{:S(2)}) copy-start(f32[256]{0:T(256)} %copy-done.6) | copy-start | bytes 3076
  231.2 65.4 %copy-start.9 = (f32[128]{0:T(128)S(1)}, f32[128]{0:T(128)}, u32[]{:S(2)}) copy-start(f32[128]{0:T(128)} %copy-done.8) | copy-start | bytes 1540
Sparse Core Ops, SparseCore 0:
  31.7 35.4 all-gather.2
  69.6 34.4 all-gather.4
  106.6 41.1 reduce-scatter.2
  150.2 43.0 reduce-scatter.4
  224.6 69.4 all-reduce.2
  296.7 300.7 all-reduce.4
